TPU v7x, 32 devices: a whole 2x2x4 slice. The times are simulated.
32 devices in a mesh: batch: 8 (over z, y), mp: 4 (over x, core).
Axes of the slice: x: 2, y: 2, z: 4, core: 2. Of those that a mesh axis runs over, the one named last changes fastest.
Arguments:
- tokens: bfloat16 [768, 128, 768], P('batch'), may hold values from -6 to 6
- lengths: int32 [768], P('batch'), may hold values from 20 to 128, as said below
- base_gains: float32 [2, 768], replicated, may hold values from 0.25 to 1.75
- base_qkv: bfloat16 [3, 768, 768], P(None, None, 'mp'), may hold values from -0.109375 to 0.109375
- base_out: bfloat16 [768, 768], replicated, may hold values from -0.75 to 0.75
- base_up: bfloat16 [768, 3072], replicated, may hold values from -0.21875 to 0.21875
- base_down: bfloat16 [3072, 768], replicated, may hold values from -0.15625 to 0.15625
- base_table: float32 [32, 12], replicated, may hold values from -4 to 4
- side_input: float32 [768, 128, 96], P(('batch', 'mp')), may hold values from -6 to 6
- output_grad: float32 [768, 128, 96], P(('batch', 'mp')), may hold values from -6 to 6
- side_weights: float32 [184320], P(('batch', 'mp'))
- weights_first: float32 [184320], P(('batch', 'mp')), may hold values from -0.00390625 to 0.00390625
- weights_second: float32 [184320], P(('batch', 'mp')), may hold values from 5.4253473e-09 to 2.170139e-08
- side_gains: float32 [3, 96], replicated
- gains_first: float32 [3, 96], replicated, may hold values from -0.0068359375 to 0.0068359375
- gains_second: float32 [3, 96], replicated, may hold values from 5.4253473e-09 to 2.7126736e-08
- side_table: float32 [32, 12], replicated, may hold values from -4 to 4
- table_first: float32 [32, 12], replicated, may hold values from -0.0014648438 to 0.0014648438
- table_second: float32 [32, 12], replicated, may hold values from 2.7126737e-10 to 1.0850695e-09
Outputs:
- side_output: float32 [768, 128, 96], P(('batch', 'mp'))
- input_grad: float32 [768, 128, 96], P(('batch', 'mp'))
- grad_norm: float32 [], replicated
- weights_moment: float32 [184320], P(('batch', 'mp'))
- weights_square: float32 [184320], P(('batch', 'mp'))
- weights_new: float32 [184320], P(('batch', 'mp'))
- weights_copy: bfloat16 [184320], P(('batch', 'mp'))
- gains_moment: float32 [3, 96], replicated
- gains_square: float32 [3, 96], replicated
- gains_new: float32 [3, 96], replicated
- table_moment: float32 [32, 12], replicated
- table_square: float32 [32, 12], replicated
- table_new: float32 [32, 12], replicated
Inputs may be any that keep to these rules, and one draw needn't show every extreme that they name: `lengths`: each sentence has 20 to 128 true tokens, and the first sentence has exactly 128.
All inputs are finite; a program needn't handle non-finite values.
Results may differ from a plain program's by a relative error of at most 0.024.
Values may be sent and summed in bfloat16 or wider, within the bound.
No kernel may reach another device: no remote copies, remote signals or barrier semaphores. Data moves between devices by JAX's collectives and lax.ppermute only.
A program may use at most 192 MiB of HBM per device.

v0:
```python
import jax
import jax.numpy as jnp
import numpy as np
from jax import lax
from jax.sharding import PartitionSpec as P

D = 768
HD = 64
DS = 96
SH = 12
SHD = 8
SFF = 384
MAXD = 128
L = 128
ADAM_STEP = 10
NORM_EPS = 1e-06
CLIP_NORM = 1.0
BETA_ONE = 0.9
BETA_TWO = 0.999
ADAM_EPS = 1e-08
RATE_MATRIX = 0.1
RATE_SMALL = 0.5
WEIGHT_DECAY = 0.01
MASKED = -1e30
PRECISE = lax.Precision.HIGHEST


def bucket_ids(length, buckets, reach):
    offset = np.arange(length)[None, :] - np.arange(length)[:, None]
    half_count = buckets // 2
    exact_count = half_count // 2
    distance = np.abs(offset)
    spread_part = (
        np.log(np.maximum(distance, 1) / exact_count)
        / np.log(reach / exact_count)
        * (half_count - exact_count)
    )
    far_bucket = np.minimum(exact_count + np.floor(spread_part).astype(np.int32), half_count - 1)
    near_side = np.where(distance < exact_count, distance, far_bucket)
    return (near_side + (offset > 0) * half_count).astype(np.int32)


def bucket_onehot(buckets):
    flat_ids = jnp.asarray(bucket_ids(L, buckets, MAXD).reshape(-1))
    return (flat_ids[:, None] == jnp.arange(buckets, dtype=jnp.int32)[None, :]).astype(jnp.float32)


def position_bias(table, onehot):
    flat_bias = jnp.dot(onehot, table, precision=PRECISE)
    return jnp.transpose(flat_bias).reshape(table.shape[1], L, L)


def rms_scale(values):
    return lax.rsqrt(jnp.mean(values * values, axis=-1, keepdims=True) + NORM_EPS)


def block_size(count):
    return min(count, max(1, 512 // L))


def masked_scores(query_blk, key_blk, length_blk, pos_bias):
    scores = (
        jnp.einsum("bqhe,bkhe->bhqk", query_blk, key_blk, preferred_element_type=jnp.float32)
        + pos_bias[None]
    )
    visible = (jnp.arange(L)[None, :] < length_blk[:, None])[:, None, None, :]
    return jnp.where(visible, scores, MASKED)


def base_attention(queries, keys_all, values_all, row_lengths, pos_bias):
    count, heads, depth = (queries.shape[0], queries.shape[2], queries.shape[3])
    block = block_size(count)
    steps_count = count // block

    def one_block(items):
        query_blk, key_blk, value_blk, length_blk = items
        scores = masked_scores(query_blk, key_blk, length_blk, pos_bias)
        row_max = jnp.max(scores, axis=-1, keepdims=True)
        exp_scores = jnp.exp(scores - row_max)
        attn_probs = (exp_scores / jnp.sum(exp_scores, axis=-1, keepdims=True)).astype(jnp.bfloat16)
        context = jnp.einsum(
            "bhqk,bkhe->bqhe", attn_probs, value_blk, preferred_element_type=jnp.float32
        )
        return context.astype(jnp.bfloat16).reshape(block, L, heads * depth)

    shaped = (
        queries.reshape(steps_count, block, L, heads, depth),
        keys_all.reshape(steps_count, block, L, heads, depth),
        values_all.reshape(steps_count, block, L, heads, depth),
        row_lengths.reshape(steps_count, block),
    )
    return lax.map(one_block, shaped).reshape(count, L, heads * depth)


def split_side(projected_blk):
    count = projected_blk.shape[0]
    return (
        projected_blk[..., :DS].reshape(count, L, SH, SHD),
        projected_blk[..., DS : 2 * DS].reshape(count, L, SH, SHD),
        projected_blk[..., 2 * DS :].reshape(count, L, SH, SHD),
    )


def side_attention(projected, row_lengths, pos_bias):
    count = projected.shape[0]
    block = block_size(count)
    steps_count = count // block

    def one_block(items):
        projected_blk, length_blk = items
        queries, keys_all, values_all = split_side(projected_blk)
        scores = masked_scores(queries, keys_all, length_blk, pos_bias)
        row_max = jnp.max(scores, axis=-1, keepdims=True)
        exp_scores = jnp.exp(scores - row_max)
        row_total = jnp.sum(exp_scores, axis=-1, keepdims=True)
        attn_probs = (exp_scores / row_total).astype(jnp.bfloat16)
        context = jnp.einsum(
            "bhqk,bkhe->bqhe", attn_probs, values_all, preferred_element_type=jnp.float32
        )
        log_total = (row_max + jnp.log(row_total))[..., 0]
        return (context.astype(jnp.bfloat16).reshape(block, L, DS), log_total)

    context, log_total = lax.map(
        one_block,
        (projected.reshape(steps_count, block, L, 3 * DS), row_lengths.reshape(steps_count, block)),
    )
    return (context.reshape(count, L, DS), log_total)


def side_attention_back(projected, grad_context, log_total, row_lengths, pos_bias):
    count = projected.shape[0]
    block = block_size(count)
    steps_count = count // block

    def one_block(items):
        projected_blk, grad_blk, log_blk, length_blk = items
        queries, keys_all, values_all = split_side(projected_blk)
        scores = masked_scores(queries, keys_all, length_blk, pos_bias)
        attn_float = jnp.exp(scores - log_blk[..., None])
        attn_low = attn_float.astype(jnp.bfloat16)
        grad_heads = grad_blk.reshape(block, L, SH, SHD)
        grad_values = jnp.einsum(
            "bhqk,bqhe->bkhe", attn_low, grad_heads, preferred_element_type=jnp.float32
        ).astype(jnp.bfloat16)
        grad_probs = jnp.einsum(
            "bqhe,bkhe->bhqk", grad_heads, values_all, preferred_element_type=jnp.float32
        )
        row_dot = jnp.sum(attn_float * grad_probs, axis=-1, keepdims=True)
        grad_scores = (attn_float * (grad_probs - row_dot)).astype(jnp.bfloat16)
        grad_queries = jnp.einsum(
            "bhqk,bkhe->bqhe", grad_scores, keys_all, preferred_element_type=jnp.float32
        ).astype(jnp.bfloat16)
        grad_keys = jnp.einsum(
            "bhqk,bqhe->bkhe", grad_scores, queries, preferred_element_type=jnp.float32
        ).astype(jnp.bfloat16)
        joined = jnp.concatenate(
            [
                grad_queries.reshape(block, L, DS),
                grad_keys.reshape(block, L, DS),
                grad_values.reshape(block, L, DS),
            ],
            axis=-1,
        )
        return (joined, jnp.sum(grad_scores.astype(jnp.float32), axis=0))

    shaped = (
        projected.reshape(steps_count, block, L, 3 * DS),
        grad_context.reshape(steps_count, block, L, DS),
        log_total,
        row_lengths.reshape(steps_count, block),
    )
    joined, bias_grad = lax.map(one_block, shaped)
    return (joined.reshape(count * L, 3 * DS), jnp.sum(bias_grad, axis=0))


def norm_back(values, scale, gain_vec, grad_normed):
    unit = values * scale
    gain_grad = jnp.sum(grad_normed * unit, axis=0)
    scaled = grad_normed * gain_vec
    return (scale * (scaled - unit * jnp.mean(scaled * unit, axis=-1, keepdims=True)), gain_grad)


def unpack(flat):
    first_end = D * DS
    second_end = first_end + 3 * DS * DS
    third_end = second_end + DS * DS
    fourth_end = third_end + DS * SFF
    return (
        flat[:first_end].reshape(D, DS),
        flat[first_end:second_end].reshape(DS, 3 * DS),
        flat[second_end:third_end].reshape(DS, DS),
        flat[third_end:fourth_end].reshape(DS, SFF),
        flat[fourth_end:].reshape(SFF, DS),
    )


def transposed_product(left, right):
    return jnp.einsum("ti,tj->ij", left, right, preferred_element_type=jnp.float32)


def back_product(left, weight):
    return jnp.einsum("tj,ij->ti", left, weight, preferred_element_type=jnp.float32)


def adamw_update(weight_now, first_now, second_now, gradient, rate, decay_rate):
    first_new = BETA_ONE * first_now + (1.0 - BETA_ONE) * gradient
    second_new = BETA_TWO * second_now + (1.0 - BETA_TWO) * gradient * gradient
    first_hat = first_new / (1.0 - BETA_ONE**ADAM_STEP)
    second_hat = second_new / (1.0 - BETA_TWO**ADAM_STEP)
    weight_new = weight_now - rate * (
        first_hat / (jnp.sqrt(second_hat) + ADAM_EPS) + decay_rate * weight_now
    )
    return (first_new, second_new, weight_new)


def on_device(
    tokens,
    lengths,
    base_gains,
    base_qkv,
    base_out,
    base_up,
    base_down,
    base_table,
    side_input,
    output_grad,
    side_weights,
    weights_first,
    weights_second,
    side_gains,
    gains_first,
    gains_second,
    side_table,
    table_first,
    table_second,
):
    model_size = lax.axis_size("mp")
    model_index = lax.axis_index("mp")
    group_seqs = tokens.shape[0]
    own_seqs = group_seqs // model_size
    own_rows = own_seqs * L
    own_tokens = lax.dynamic_slice_in_dim(tokens, model_index * own_seqs, own_seqs, 0)
    own_lengths = lax.dynamic_slice_in_dim(lengths, model_index * own_seqs, own_seqs, 0)
    weights_low = lax.all_gather(
        side_weights.astype(jnp.bfloat16), ("batch", "mp"), axis=0, tiled=True
    )
    base_onehot = bucket_onehot(base_table.shape[0])
    own_float = own_tokens.reshape(own_rows, D).astype(jnp.float32)
    local_heads = base_qkv.shape[2] // HD
    group_float = tokens.reshape(group_seqs * L, D).astype(jnp.float32)
    normed = (group_float * rms_scale(group_float) * base_gains[0]).astype(jnp.bfloat16)
    projected = jnp.einsum(
        "td,kdc->ktc", normed, base_qkv, preferred_element_type=jnp.float32
    ).astype(jnp.bfloat16)
    table_part = lax.dynamic_slice_in_dim(base_table, model_index * local_heads, local_heads, 1)
    pieces = projected.reshape(3, group_seqs, L, local_heads, HD)
    context = base_attention(
        pieces[0], pieces[1], pieces[2], lengths, position_bias(table_part, base_onehot)
    )
    context = lax.all_to_all(context, "mp", split_axis=0, concat_axis=2, tiled=True)
    base_middle = own_float + jnp.dot(
        context.reshape(own_rows, D), base_out, preferred_element_type=jnp.float32
    )
    base_normed = (base_middle * rms_scale(base_middle) * base_gains[1]).astype(jnp.bfloat16)
    base_hidden = jax.nn.gelu(
        jnp.dot(base_normed, base_up, preferred_element_type=jnp.float32)
    ).astype(jnp.bfloat16)
    taps = (
        base_middle + jnp.dot(base_hidden, base_down, preferred_element_type=jnp.float32)
    ).astype(jnp.bfloat16)
    w_down, w_qkv, w_out, w_up, w_back = unpack(weights_low)
    side_rows = side_input.reshape(own_rows, DS)
    keep_rows = (
        (jnp.arange(L)[None, :] < own_lengths[:, None]).astype(jnp.float32).reshape(own_rows, 1)
    )
    grad_out = output_grad.reshape(own_rows, DS) * keep_rows
    mixing = jax.nn.sigmoid(side_gains[2])
    tapped = jnp.dot(taps, w_down, preferred_element_type=jnp.float32)
    mixed = mixing * side_rows + (1.0 - mixing) * tapped
    scale_one = rms_scale(mixed)
    normed_one = (mixed * scale_one * side_gains[0]).astype(jnp.bfloat16)
    projected_side = jnp.dot(normed_one, w_qkv, preferred_element_type=jnp.float32).astype(
        jnp.bfloat16
    )
    side_onehot = bucket_onehot(side_table.shape[0])
    side_bias = position_bias(side_table, side_onehot)
    projected_seq = projected_side.reshape(own_seqs, L, 3 * DS)
    context_side, log_total = side_attention(projected_seq, own_lengths, side_bias)
    context_flat = context_side.reshape(own_rows, DS)
    middle = mixed + jnp.dot(context_flat, w_out, preferred_element_type=jnp.float32)
    scale_two = rms_scale(middle)
    normed_two = (middle * scale_two * side_gains[1]).astype(jnp.bfloat16)
    pre_act = jnp.dot(normed_two, w_up, preferred_element_type=jnp.float32)
    activated, gelu_back = jax.vjp(jax.nn.gelu, pre_act)
    hidden = activated.astype(jnp.bfloat16)
    side_output = middle + jnp.dot(hidden, w_back, preferred_element_type=jnp.float32)
    grad_low = grad_out.astype(jnp.bfloat16)
    grad_back = transposed_product(hidden, grad_low)
    grad_pre = gelu_back(back_product(grad_low, w_back))[0].astype(jnp.bfloat16)
    grad_up = transposed_product(normed_two, grad_pre)
    grad_normed_two = back_product(grad_pre, w_up)
    norm_part, gain_two_grad = norm_back(middle, scale_two, side_gains[1], grad_normed_two)
    grad_middle = grad_out + norm_part
    grad_attended = grad_middle.astype(jnp.bfloat16)
    grad_out_proj = transposed_product(context_flat, grad_attended)
    grad_context = back_product(grad_attended, w_out).astype(jnp.bfloat16)
    grad_qkv, bias_grad = side_attention_back(
        projected_seq, grad_context.reshape(own_seqs, L, DS), log_total, own_lengths, side_bias
    )
    table_grad = jnp.einsum(
        "hp,pn->nh", bias_grad.reshape(SH, L * L), side_onehot, precision=PRECISE
    )
    grad_qkv_weight = transposed_product(normed_one, grad_qkv)
    grad_normed_one = back_product(grad_qkv, w_qkv)
    norm_part_one, gain_one_grad = norm_back(mixed, scale_one, side_gains[0], grad_normed_one)
    grad_mixed = grad_middle + norm_part_one
    input_grad = mixing * grad_mixed
    grad_tap = ((1.0 - mixing) * grad_mixed).astype(jnp.bfloat16)
    grad_down = transposed_product(taps, grad_tap)
    gate_grad = jnp.sum(grad_mixed * (side_rows - tapped), axis=0) * mixing * (1.0 - mixing)
    flat_grad = jnp.concatenate(
        [
            grad_down.reshape(-1),
            grad_qkv_weight.reshape(-1),
            grad_out_proj.reshape(-1),
            grad_up.reshape(-1),
            grad_back.reshape(-1),
        ]
    )
    grad_shard = lax.psum_scatter(flat_grad, ("batch", "mp"), scatter_dimension=0, tiled=True)
    gains_part = jnp.stack([gain_one_grad, gain_two_grad, gate_grad])
    gains_total, table_total, square_total = lax.psum(
        (gains_part, table_grad, jnp.sum(grad_shard * grad_shard)), ("batch", "mp")
    )
    grad_norm = jnp.sqrt(
        square_total + jnp.sum(gains_total * gains_total) + jnp.sum(table_total * table_total)
    )
    factor = CLIP_NORM / jnp.maximum(grad_norm, CLIP_NORM)
    weights_moment, weights_square, weights_new = adamw_update(
        side_weights, weights_first, weights_second, factor * grad_shard, RATE_MATRIX, WEIGHT_DECAY
    )
    gains_moment, gains_square, gains_new = adamw_update(
        side_gains, gains_first, gains_second, factor * gains_total, RATE_SMALL, 0.0
    )
    table_moment, table_square, table_new = adamw_update(
        side_table, table_first, table_second, factor * table_total, RATE_SMALL, 0.0
    )
    return (
        side_output.reshape(own_seqs, L, DS),
        input_grad.reshape(own_seqs, L, DS),
        grad_norm,
        weights_moment,
        weights_square,
        weights_new,
        weights_new.astype(jnp.bfloat16),
        gains_moment,
        gains_square,
        gains_new,
        table_moment,
        table_square,
        table_new,
    )


def solution(mesh):
    return jax.shard_map(
        on_device,
        mesh=mesh,
        in_specs=(
            P("batch", None, None),
            P("batch"),
            P(),
            P(None, None, "mp"),
            P(),
            P(),
            P(),
            P(),
            P(("batch", "mp"), None, None),
            P(("batch", "mp"), None, None),
            P(("batch", "mp")),
            P(("batch", "mp")),
            P(("batch", "mp")),
            P(),
            P(),
            P(),
            P(),
            P(),
            P(),
        ),
        out_specs=(
            P(("batch", "mp"), None, None),
            P(("batch", "mp"), None, None),
            P(),
            P(("batch", "mp")),
            P(("batch", "mp")),
            P(("batch", "mp")),
            P(("batch", "mp")),
            P(),
            P(),
            P(),
            P(),
            P(),
            P(),
        ),
        check_vma=False,
    )
```

profile of v0, /device:TPU:0, one launch (start us, length us, event | category | flops | bytes accessed | tf_op | source)
XLA Modules:
  0.0 765.9 jit_solution(16169485788570757900)
XLA Ops:
  8.1 8.7 %multiply_reduce_fusion.1 = f32[96,128]{1,0:T(8,128)S(1)} fusion(bf16[96,128,768]{2,1,0:T(8,128)(2,1)} %param.27), kind=kLoop, calls=%fused_computation.77 | loop fusion | flops 28299264 | bytes 18923520 | tf_op jit(solution)/shard_map/reduce_sum | solution.py:54
  16.7 3.3 copy-done.2
  20.1 10.1 %fusion.36 = bf16[12288,768]{1,0:T(8,128)(2,1)} fusion(f32[768]{0:T(1024)S(1)} %get-tuple-element.374, f32[12288]{0:T(1024)S(1)} %rsqrt_bitcast_fusion, bf16[96,128,768]{2,1,0:T(8,128)(2,1)S(1)} %copy-done.2), kind=kLoop, calls=%fused_computation.76 | loop fusion | flops 37748736 | bytes 37800960 | tf_op jit(solution)/shard_map/convert_element_type | solution.py:251
  30.1 34.4 %fusion.94 = f32[12288,576]{0,1} fusion(bf16[12288,768]{1,0:T(8,128)(2,1)} %fusion.36, bf16[768,576]{0,1:T(8,128)(2,1)S(1)} %bitcast.320), kind=kOutput, calls=%fused_computation.190 | convolution fusion | flops 10871635968 | bytes 48070656
  64.5 10.5 %convert_bitcast_fusion = bf16[3,12288,192]{1,2,0:T(8,128)(2,1)S(1)} fusion(f32[12288,3,192]{0,2,1:T(8,128)} %bitcast.306), kind=kLoop, calls=%fused_computation.80 | loop fusion | flops 7077888 | bytes 42467328 | tf_op jit(solution)/shard_map/convert_element_type | solution.py:254
  75.1 5.1 fusion.92
  80.2 8.1 %reshape_squeeze.10 = bf16[24,4,128,3,64]{2,1,0,4,3:T(4,128)(2,1)} reshape(bf16[1,12288,192]{1,2,0:T(8,128)(2,1)} %get-tuple-element.445) | data formatting | bytes 9437184 | tf_op jit(solution)/shard_map/reshape;squeeze | solution.py:87
  88.3 8.2 %reshape_squeeze.11 = bf16[24,4,128,3,64]{2,1,0,4,3:T(4,128)(2,1)} reshape(bf16[1,12288,192]{1,2,0:T(8,128)(2,1)} %get-tuple-element.444) | data formatting | bytes 9437184 | tf_op jit(solution)/shard_map/reshape;squeeze | solution.py:88
  96.5 8.2 %reshape_squeeze.9 = bf16[24,4,128,3,64]{2,1,0,4,3:T(4,128)(2,1)} reshape(bf16[1,12288,192]{1,2,0:T(8,128)(2,1)} %get-tuple-element.446) | data formatting | bytes 9437184 | tf_op jit(solution)/shard_map/reshape;squeeze | solution.py:89
  104.8 1.4 fusion.56
  106.2 103.0 %while.34 = (s32[]{:T(128)}, bf16[24,4,128,192]{2,3,1,0:T(8,128)(2,1)}, bf16[24,4,128,3,64]{2,1,0,4,3:T(4,128)(2,1)}, s32[24,4]{1,0:T(8,128)S(1)}, bf16[24,4,128...) while((s32[]{:T(128)}, ...), condition=%wide.region_4.5_spmd, body=%wide.region_1.4_spmd.sunk | while | flops 77367552 | bytes 5519505 | solution.py:92
  209.2 5.1 all-to-all-start
  214.4 90.6 %all-gather = bf16[32,1,5760]{2,1,0:T(2,128)(2,1)S(1)} all-gather(bf16[1,1,5760]{2,1,0:T(2,128)(2,1)S(1)} %reshape.349), channel_id=1, replica_groups=mesh['batch'=8,'mp'=4] {'batch','mp'}, dimensions={0}, use_global_device_ids=true | all-gather | bytes 380160 | tf_op jit(solution)/shard_map/all_gather | solution.py:244
  305.0 2.2 reduce.2
  307.8 2.8 constant_dynamic-slice_fusion.7
  310.6 4.7 bitcast_convert_fusion
  315.3 9.7 %copy.213 = f32[3072,768]{0,1:T(8,128)} copy(f32[3072,768]{1,0:T(8,128)} %bitcast_convert_fusion) | data formatting | bytes 18874368 | tf_op jit(solution)/shard_map/convert_element_type | solution.py:248
  325.9 1.7 convolution_bitcast_fusion
  327.6 5.5 copy.192
  333.2 6.9 multiply_reduce_fusion.2
  340.1 42.9 %add_convert_fusion = bf16[3072,768]{0,1:T(8,128)(2,1)} fusion(f32[3072,768]{0,1:T(8,128)} %get-tuple-element.454, bf16[3072,768]{1,0:T(8,128)(2,1)} %param.33, bf16[768,3072]{1,0:T(8,128)(2,1)} %param.32, f32[768]{0:T(1024)S(1)} %get-tuple-element.373, f32[3072]{0:T(1024)S(1)} %add_rsqrt_fusion.2), kind=kOutput, calls=%fused_computation.81 | convolution fusion | flops 29087760384 | bytes 23608320 | tf_op jit(solution)/shard_map/dot_general | solution.py:269
  383.0 4.4 multiply_reduce_fusion.8
  387.4 1.9 convolution_convert_fusion.3
  389.4 4.4 reshape_reshape.10
  393.8 3.0 copy.194
  396.8 42.3 %while.35 = (s32[]{:T(128)}, bf16[6,4,128,96]{2,1,0,3:T(4,128)(2,1)}, f32[6,4,12,128]{3,2,1,0:T(8,128)}, bf16[6,4,128,288]{2,3,1,0:T(8,128)(2,1)}, s32[6,4]{1,0:T(8,128)S(1)}, /*index=5*/f32[12,16384]{1,0:T(8,128)}, s32[]{:T(128)}) while((s32[]{:T(128)}, bf16[6,4,128,96]{2,1,0,3:T(4,128)(2,1)}, f32[6,4,12,128]{3,2,1,0:T(8,128)}, ...), condition=%wide.region_10.11_spmd, body=%wide.region_7.10_spmd.sunk | while | flops 34646528 | bytes 18443396 | solution.py:123
  398.0 1.4 copy.293
  405.1 1.4 copy.293
  412.1 1.4 copy.293
  419.1 1.4 copy.293
  426.1 1.4 copy.293
  433.2 1.4 copy.293
  439.1 1.5 reshape_reshape.11
  442.8 3.6 fusion.47
  446.4 1.5 multiply_reduce_fusion.3
  451.9 103.6 %while.36 = (s32[]{:T(128)}, bf16[6,4,128,288]{2,1,0,3:T(4,128)(2,1)}, f32[6,12,128,128]{2,3,1,0:T(8,128)}, bf16[6,4,128,288]{2,3,1,0:T(8,128)(2,1)}, s32[6,4]{1...) while((s32[]{:T(128)}, ...), condition=%wide.region_16.17_spmd, body=%wide.region_13.16_spmd.sunk | while | flops 72395264 | bytes 39775244 | solution.py:172
  456.9 1.4 copy.298
  459.2 2.3 copy.299
  461.6 2.5 multiply_reduce_fusion.13
  474.2 1.4 copy.298
  476.5 2.3 copy.299
  478.8 2.5 multiply_reduce_fusion.13
  491.4 1.4 copy.298
  493.8 2.3 copy.299
  496.1 2.5 multiply_reduce_fusion.13
  508.7 1.4 copy.298
  511.1 2.3 copy.299
  513.4 2.5 multiply_reduce_fusion.13
  528.3 2.3 copy.299
  530.6 2.5 multiply_reduce_fusion.13
  545.6 2.3 copy.299
  547.9 2.5 multiply_reduce_fusion.13
  555.5 3.4 reshape.338
  558.9 2.3 multiply_reduce_fusion.4
  562.0 5.2 fusion.70
  567.3 2.9 fusion.57
  573.0 3.1 fusion.60
  576.0 3.8 fusion.65
  581.9 2.8 reduce_sum.167
  587.0 118.5 %all-reduce.4.cloned.1.call-done = f32[184320]{0:T(1024)} async-done(((f32[184320]{0:T(1024)}), f32[184320]{0:T(1024)}) %all-reduce.4.cloned.1.call-update) | async-done | bytes 737296
  705.5 1.4 multiply_reduce_fusion.9
  706.9 2.9 copy_bitcast_fusion.14
  709.8 40.5 %all-reduce.1 = (f32[]{:T(128)}, f32[3,96]{1,0:T(4,128)S(1)}, f32[32,12]{0,1:T(8,128)S(1)}) all-reduce(f32[]{:T(128)} %multiply_reduce_fusion.9, f32[3,96]{1,0:T(4,128)S(1)} %pad_maximum_fusion, f32[32,12]{0,1:T(8,128)S(1)} %fusion.55), channel_id=1, replica_groups=mesh['batch'=8,'mp'=4] {'batch','mp'}, use_global_device_ids=true, to_apply=%region_20.21 | all-reduce | flops 673 | bytes 5384 | tf_op jit(solution)/shard_map/psum | solution.py:332
  756.3 1.5 fusion.88
  (597 shorter events, 224.0 us)
Async XLA Ops:
  7.2 326.0 %copy-start = (bf16[768,768]{1,0:T(8,128)(2,1)S(1)}, bf16[768,768]{1,0:T(8,128)(2,1)}, u32[]{:S(2)}) copy-start(bf16[768,768]{1,0:T(8,128)(2,1)} %param.31) | copy-start | bytes 3538948
  8.0 12.0 %copy-start.2 = (bf16[96,128,768]{2,1,0:T(8,128)(2,1)S(1)}, bf16[96,128,768]{2,1,0:T(8,128)(2,1)}, u32[]{:S(2)}) copy-start(bf16[96,128,768]{2,1,0:T(8,128)(2,1)} %param.27) | copy-start | bytes 56623108
  20.1 10.1 %copy-start.51 = (bf16[3,768,192]{1,2,0:T(8,128)(2,1)S(1)}, bf16[3,768,192]{1,2,0:T(8,128)(2,1)}, u32[]{:S(2)}) copy-start(bf16[3,768,192]{1,2,0:T(8,128)(2,1)} %param.30) | copy-start | bytes 2654212
  96.5 8.2 %copy-start.49 = (s32[96]{0:T(128)S(1)}, s32[96]{0:T(128)}, u32[]{:S(2)}) copy-start(s32[96]{0:T(128)} %param.28) | copy-start | bytes 1156
  96.5 8.3 %copy-start.24 = (s32[16384]{0:T(1024)S(1)}, s32[16384]{0:T(1024)}, u32[]{:S(2)}) copy-start(s32[16384]{0:T(1024)} %constant.88.clone) | copy-start | bytes 196612
  209.2 5.1 copy-start.31
  209.2 118.4 %all-to-all-start = ((bf16[96,128,192]{1,2,0:T(8,128)(2,1)}), bf16[96,128,192]{1,2,0:T(8,128)(2,1)}, u32[]{:S(2)}, u32[]{:S(2)}) async-start(bf16[96,128,192]{1,2,0:T(8,128)(2,1)} %bitcast.310), calls=%async_computation | async-start | bytes 9437184 | tf_op jit(solution)/shard_map/all_to_all | solution.py:260
  214.3 491.2 %all-reduce.4.cloned.1.call-start = ((), (), s32[]{:S(2)}) async-start(), calls=%async_computation.1 | async-start | bytes 1474560
  307.7 2.9 copy-start.14
  315.3 9.8 %slice-start.2 = ((bf16[184320]{0:T(1024)(128)(2,1)}), bf16[73728]{0:T(1024)(128)(2,1)S(1)}, s32[]{:S(2)}) async-start(bf16[184320]{0:T(1024)(128)(2,1)} %copy-done.14), calls=%async_computation.4 | async-start | bytes 294912 | tf_op jit(solution)/shard_map/slice | solution.py:189
  315.3 9.9 %slice-start.3 = ((bf16[184320]{0:T(1024)(128)(2,1)}), bf16[27648]{0:T(1024)(128)(2,1)S(1)}, s32[]{:S(2)}) async-start(bf16[184320]{0:T(1024)(128)(2,1)} %copy-done.14), calls=%async_computation.5 | async-start | bytes 110592 | tf_op jit(solution)/shard_map/slice | solution.py:190
  315.3 10.2 %slice-start.4 = ((bf16[184320]{0:T(1024)(128)(2,1)}), bf16[9216]{0:T(1024)(128)(2,1)S(1)}, s32[]{:S(2)}) async-start(bf16[184320]{0:T(1024)(128)(2,1)} %copy-done.14), calls=%async_computation.6 | async-start | bytes 36864 | tf_op jit(solution)/shard_map/slice | solution.py:191
  315.3 10.3 %copy-start.15 = (bf16[184320]{0:T(1024)(128)(2,1)S(1)}, bf16[184320]{0:T(1024)(128)(2,1)}, u32[]{:S(2)}) copy-start(bf16[184320]{0:T(1024)(128)(2,1)} %copy-done.14) | copy-start | bytes 1105924
  315.3 10.5 %copy-start.43 = (f32[3,96]{1,0:T(4,128)S(1)}, f32[3,96]{1,0:T(4,128)}, u32[]{:S(2)}) copy-start(f32[3,96]{1,0:T(4,128)} %param.40) | copy-start | bytes 3460
  315.3 10.6 %copy-start.35 = (f32[32,12]{0,1:T(8,128)S(1)}, f32[32,12]{0,1:T(8,128)}, u32[]{:S(2)}) copy-start(f32[32,12]{0,1:T(8,128)} %param.43) | copy-start | bytes 4612
  325.4 62.1 %copy-start.19 = (bf16[96,288]{1,0:T(8,128)(2,1)}, bf16[96,288]{1,0:T(8,128)(2,1)S(1)}, u32[]{:S(2)}) copy-start(bf16[96,288]{1,0:T(8,128)(2,1)S(1)} %slice.122) | copy-start | bytes 165892
  325.8 116.2 %copy-start.29 = (bf16[384,96]{1,0:T(8,128)(2,1)}, bf16[384,96]{1,0:T(8,128)(2,1)S(1)}, u32[]{:S(2)}) copy-start(bf16[384,96]{1,0:T(8,128)(2,1)S(1)} %slice.129) | copy-start | bytes 221188
  325.8 57.2 %copy-start.38 = (f32[1,96]{1,0:T(1,128)}, f32[1,96]{1,0:T(1,128)S(1)}, u32[]{:S(2)}) copy-start(f32[1,96]{1,0:T(1,128)S(1)} %get-tuple-element.452) | copy-start | bytes 1156
  325.8 57.2 %copy-start.40 = (f32[96]{0:T(128)}, f32[96]{0:T(128)S(1)}, u32[]{:S(2)}) copy-start(f32[96]{0:T(128)S(1)} %get-tuple-element.451) | copy-start | bytes 1156
  325.9 123.2 %copy-start.33 = (f32[3072]{0:T(1024)}, f32[3072]{0:T(1024)S(1)}, u32[]{:S(2)}) copy-start(f32[3072]{0:T(1024)S(1)} %convert_bitcast_fusion.1) | copy-start | bytes 36868
  327.6 5.5 copy-start.9
  340.1 42.9 %copy-start.10 = (f32[24,128,96]{1,2,0:T(8,128)S(1)}, f32[24,128,96]{1,2,0:T(8,128)}, u32[]{:S(2)}) copy-start(f32[24,128,96]{1,2,0:T(8,128)} %param.35) | copy-start | bytes 3538948
  387.4 53.2 %copy-start.3 = (f32[3072,96]{0,1:T(8,128)}, f32[3072,96]{0,1:T(8,128)S(1)}, u32[]{:S(2)}) copy-start(f32[3072,96]{0,1:T(8,128)S(1)} %get-tuple-element.435) | copy-start | bytes 3538948
  441.0 8.1 %copy-start.5 = (f32[3072,96]{0,1:T(8,128)}, f32[3072,96]{0,1:T(8,128)S(1)}, u32[]{:S(2)}) copy-start(f32[3072,96]{0,1:T(8,128)S(1)} %get-tuple-element.457) | copy-start | bytes 3538948
  441.1 1.7 copy-start.17
  442.8 3.6 copy-start.11
  466.4 2.8 copy-start.13
  467.3 1.9 copy-start.45
  469.2 1.6 copy-start.12
  483.7 2.9 copy-start.13
  484.6 1.9 copy-start.45
  486.5 1.6 copy-start.12
  500.9 2.8 copy-start.13
  501.9 1.9 copy-start.45
  503.8 1.6 copy-start.12
  518.2 2.8 copy-start.13
  519.1 1.9 copy-start.45
  521.0 1.6 copy-start.12
  535.5 2.8 copy-start.13
  536.4 1.9 copy-start.45
  538.3 1.6 copy-start.12
  552.7 2.8 copy-start.13
  553.6 1.9 copy-start.45
  555.5 3.4 copy-start.4
  555.5 3.4 copy-start.20
  558.9 3.1 copy-start.18
  558.9 3.1 copy-start.34
  561.2 6.0 slice-start
  562.0 5.2 copy-start.6
  562.0 5.2 slice-start.1
  562.0 5.2 copy-start.30
  567.2 3.5 copy-start.21
  567.3 4.2 copy-start.27
  567.3 5.7 copy-start.8
  572.9 3.1 copy-start.41
  576.0 4.2 copy-start.26
  576.0 4.3 copy-start.23
  576.0 4.3 copy-start.28
  576.0 4.4 copy-start.22
  585.1 172.6 %copy-start.1 = (bf16[768,768]{1,0:T(8,128)(2,1)S(1)}, bf16[768,768]{1,0:T(8,128)(2,1)}, u32[]{:S(2)}) copy-start(bf16[768,768]{1,0:T(8,128)(2,1)} %param.31) | copy-start | bytes 3538948
  585.7 167.9 %copy-start.36 = (f32[32,12]{0,1:T(8,128)S(1)}, f32[32,12]{0,1:T(8,128)}, u32[]{:S(2)}) copy-start(f32[32,12]{0,1:T(8,128)} %param.43) | copy-start | bytes 4612
  585.8 167.9 %copy-start.42 = (f32[32,12]{0,1:T(8,128)S(1)}, f32[32,12]{0,1:T(8,128)}, u32[]{:S(2)}) copy-start(f32[32,12]{0,1:T(8,128)} %param.45) | copy-start | bytes 4612
  585.8 170.5 %copy-start.32 = (f32[5760]{0:T(1024)S(1)}, f32[5760]{0:T(1024)}, u32[]{:S(2)}) copy-start(f32[5760]{0:T(1024)} %param.37) | copy-start | bytes 69124
  585.8 170.5 %copy-start.37 = (f32[5760]{0:T(1024)S(1)}, f32[5760]{0:T(1024)}, u32[]{:S(2)}) copy-start(f32[5760]{0:T(1024)} %param.39) | copy-start | bytes 69124
  (15 other events, 14.0 us)
Sparse Core Ops, SparseCore 0:
  581.4 123.9 all-reduce.3
where the time goes:
time: 777 us; the launch traced here: 766 us
  local copies, waits for them, and re-layouts  227 us (29%)
  matrix products  191 us (25%)
  blocking collectives  131 us (17%)
  waiting for transfers between devices  118 us (15%)
  other arithmetic  73.6 us (9%)
  between operations  18.3 us (2%)
    unnamed x2, waiting for transfers between devices  118 us
    all_gather x1, blocking collectives, on_device(): lax.all_gather(side_weights.astype(jnp.bfloat16), ('batch', 'mp'), axis=0...  90.6 us
    dynamic_slice x48, local copies, waits for them, and re-layouts, base_attention(): return lax.map(one_block, shaped).reshape(count, L, heads * depth)  52.2 us
    dot_general x1, matrix products, on_device(): jnp.dot(base_hidden, base_down, preferred_element_type=jnp.float32)  42.9 us
    psum x1, blocking collectives, on_device(): lax.psum((gains_part, table_grad, jnp.sum(grad_shard * grad_shard)), ('ba...  40.5 us
    unnamed x1, matrix products  34.4 us
    dot_general x36, matrix products, masked_scores(): jnp.einsum('bqhe,bkhe->bhqk', query_blk, key_blk, preferred_element_type=...  29.4 us
    add x48, local copies, waits for them, and re-layouts, masked_scores(): jnp.einsum('bqhe,bkhe->bhqk', query_blk, key_blk, preferred_element_type=...  24.5 us
  transfers between devices with their start and end apart: 2, of which 1 were waited for; matrix products, arithmetic and copies ran while one was open for 4% of the time, Pallas kernels for 0%

commit v1 on v0

--- a/solution.py
+++ b/solution.py
@@ -241,9 +241,16 @@
     own_rows = own_seqs * L
     own_tokens = lax.dynamic_slice_in_dim(tokens, model_index * own_seqs, own_seqs, 0)
     own_lengths = lax.dynamic_slice_in_dim(lengths, model_index * own_seqs, own_seqs, 0)
-    weights_low = lax.all_gather(
-        side_weights.astype(jnp.bfloat16), ("batch", "mp"), axis=0, tiled=True
-    )
+    x = side_weights.astype(jnp.bfloat16)
+    ways, here = (lax.axis_size(("batch", "mp")), lax.axis_index(("batch", "mp")))
+    grown, reach_2 = (x, 1)
+    while reach_2 < ways:
+        theirs = lax.ppermute(grown, ("batch", "mp"), [(d, d ^ reach_2) for d in range(ways)])
+        mine_first = jnp.concatenate([grown, theirs], axis=0)
+        theirs_first = jnp.concatenate([theirs, grown], axis=0)
+        grown = jnp.where(here & reach_2 == 0, mine_first, theirs_first)
+        reach_2 = 2 * reach_2
+    weights_low = grown
     base_onehot = bucket_onehot(base_table.shape[0])
     own_float = own_tokens.reshape(own_rows, D).astype(jnp.float32)
     local_heads = base_qkv.shape[2] // HD

time: 777 us -> 743 us (0.956)
  blocking collectives: 131 us -> 40.5 us
  waiting for transfers between devices: 118 us -> 164 us
  starting transfers between devices: 5.1 us -> 14.5 us
    all_gather x1 -> x0, blocking collectives: 90.6 us -> none  [on_device(): lax.all_gather(side_weights.astype(jnp.bfloat16), ('batch', 'mp'), axis=0...]
    ppermute x0 -> x5, waiting for transfers between devices: none -> 41.4 us  [on_device(): lax.ppermute(grown, ('batch', 'mp'), [(d, d ^ reach_2) for d in range(way...]
    ppermute x0 -> x5, starting transfers between devices: none -> 9.34 us  [on_device(): lax.ppermute(grown, ('batch', 'mp'), [(d, d ^ reach_2) for d in range(way...]
    while x84 -> x60, local copies, waits for them, and re-layouts: 21 us -> 17.5 us
  transfers between devices with their start and end apart: 2 -> 7, of which waited for: 1 -> 5; matrix products, arithmetic and copies ran while one was open for 4% -> 31% of each run, Pallas kernels for 0% -> 0%
where the time goes in v1:
time: 743 us; the launch traced here: 732 us
  local copies, waits for them, and re-layouts  229 us (31%)
  matrix products  192 us (26%)
  waiting for transfers between devices  164 us (22%)
  other arithmetic  71.6 us (10%)
  blocking collectives  40.5 us (5%)
  between operations  18.3 us (2%)
  starting transfers between devices  14.5 us (2%)
    unnamed x2, waiting for transfers between devices  123 us
    dynamic_slice x48, local copies, waits for them, and re-layouts, base_attention(): return lax.map(one_block, shaped).reshape(count, L, heads * depth)  52.2 us
    dot_general x1, matrix products, on_device(): jnp.dot(base_hidden, base_down, preferred_element_type=jnp.float32)  42.8 us
    ppermute x5, waiting for transfers between devices, on_device(): lax.ppermute(grown, ('batch', 'mp'), [(d, d ^ reach_2) for d in range(way...  41.4 us
    psum x1, blocking collectives, on_device(): lax.psum((gains_part, table_grad, jnp.sum(grad_shard * grad_shard)), ('ba...  40.5 us
    unnamed x1, matrix products  34.4 us
    dot_general x36, matrix products, masked_scores(): jnp.einsum('bqhe,bkhe->bhqk', query_blk, key_blk, preferred_element_type=...  29.4 us
    add x48, local copies, waits for them, and re-layouts, masked_scores(): jnp.einsum('bqhe,bkhe->bhqk', query_blk, key_blk, preferred_element_type=...  24.4 us
  transfers between devices with their start and end apart: 7, of which 5 were waited for; matrix products, arithmetic and copies ran while one was open for 31% of the time, Pallas kernels for 0%

profile of v1, /device:TPU:0, one launch (start us, length us, event | category | flops | bytes accessed | tf_op | source)
XLA Modules:
  0.0 732.1 jit_solution(15675335549168006652)
XLA Ops:
  9.3 8.7 %multiply_reduce_fusion.1 = f32[96,128]{1,0:T(8,128)S(1)} fusion(bf16[96,128,768]{2,1,0:T(8,128)(2,1)} %param.27), kind=kLoop, calls=%fused_computation.77 | loop fusion | flops 28299264 | bytes 18923520 | tf_op jit(solution)/shard_map/reduce_sum | solution.py:54
  18.0 3.3 copy-done.2
  21.3 10.2 %fusion.36 = bf16[12288,768]{1,0:T(8,128)(2,1)} fusion(f32[768]{0:T(1024)S(1)} %get-tuple-element.374, f32[12288]{0:T(1024)S(1)} %rsqrt_bitcast_fusion, bf16[96,128,768]{2,1,0:T(8,128)(2,1)S(1)} %copy-done.2), kind=kLoop, calls=%fused_computation.76 | loop fusion | flops 37748736 | bytes 37800960 | tf_op jit(solution)/shard_map/convert_element_type | solution.py:258
  31.5 34.4 %fusion.101 = f32[12288,576]{0,1} fusion(bf16[12288,768]{1,0:T(8,128)(2,1)} %fusion.36, bf16[768,576]{0,1:T(8,128)(2,1)S(1)} %bitcast.315), kind=kOutput, calls=%fused_computation.215 | convolution fusion | flops 10871635968 | bytes 48070656
  65.9 10.5 %convert_bitcast_fusion = bf16[3,12288,192]{1,2,0:T(8,128)(2,1)S(1)} fusion(f32[12288,3,192]{0,2,1:T(8,128)} %bitcast.301), kind=kLoop, calls=%fused_computation.80 | loop fusion | flops 7077888 | bytes 42467328 | tf_op jit(solution)/shard_map/convert_element_type | solution.py:261
  76.4 5.1 fusion.100
  81.5 8.1 %reshape_squeeze.10 = bf16[24,4,128,3,64]{2,1,0,4,3:T(4,128)(2,1)} reshape(bf16[1,12288,192]{1,2,0:T(8,128)(2,1)} %get-tuple-element.445) | data formatting | bytes 9437184 | tf_op jit(solution)/shard_map/reshape;squeeze | solution.py:87
  89.6 8.2 %reshape_squeeze.11 = bf16[24,4,128,3,64]{2,1,0,4,3:T(4,128)(2,1)} reshape(bf16[1,12288,192]{1,2,0:T(8,128)(2,1)} %get-tuple-element.444) | data formatting | bytes 9437184 | tf_op jit(solution)/shard_map/reshape;squeeze | solution.py:88
  97.8 8.2 %reshape_squeeze.9 = bf16[24,4,128,3,64]{2,1,0,4,3:T(4,128)(2,1)} reshape(bf16[1,12288,192]{1,2,0:T(8,128)(2,1)} %get-tuple-element.446) | data formatting | bytes 9437184 | tf_op jit(solution)/shard_map/reshape;squeeze | solution.py:89
  106.1 1.4 fusion.56
  107.5 102.8 %while.34 = (s32[]{:T(128)}, bf16[24,4,128,192]{2,3,1,0:T(8,128)(2,1)}, bf16[24,4,128,3,64]{2,1,0,4,3:T(4,128)(2,1)}, s32[24,4]{1,0:T(8,128)S(1)}, bf16[24,4,128...) while((s32[]{:T(128)}, ...), condition=%wide.region_4.5_spmd, body=%wide.region_1.4_spmd.sunk | while | flops 77367552 | bytes 5519505 | solution.py:92
  210.4 4.9 all-to-all-start
  215.5 2.8 constant_dynamic-slice_fusion.7
  218.4 4.7 bitcast_convert_fusion
  223.1 1.7 convolution_bitcast_fusion
  225.5 2.5 collective-permute-start.1
  229.3 9.7 %copy.213 = f32[3072,768]{0,1:T(8,128)} copy(f32[3072,768]{1,0:T(8,128)} %bitcast_convert_fusion) | data formatting | bytes 18874368 | tf_op jit(solution)/shard_map/convert_element_type | solution.py:255
  239.1 31.3 %collective-permute-done.1 = bf16[11520]{0:T(1024)(128)(2,1)S(1)} collective-permute-done((bf16[11520]{0:T(1024)(128)(2,1)S(1)}, bf16[11520]{0:T(1024)(128)(2,1)S(1)}, u32[]{:S(2)}, u32[]{:S(2)}) %collective-permute-start.1) | collective-permute-done | bytes 23072 | tf_op jit(solution)/shard_map/ppermute | solution.py:248
  270.5 1.7 collective-permute-start.2
  272.5 2.1 collective-permute-done.2
  274.6 1.8 collective-permute-start.3
  276.8 2.4 collective-permute-done.3
  279.3 2.8 collective-permute-start.4
  282.7 5.7 collective-permute-done.4
  290.0 5.6 copy.192
  295.6 7.0 multiply_reduce_fusion.2
  302.5 42.8 %add_convert_fusion = bf16[3072,768]{0,1:T(8,128)(2,1)} fusion(f32[3072,768]{0,1:T(8,128)} %get-tuple-element.452, bf16[3072,768]{1,0:T(8,128)(2,1)} %param.33, bf16[768,3072]{1,0:T(8,128)(2,1)} %param.32, f32[768]{0:T(1024)S(1)} %get-tuple-element.373, f32[3072]{0:T(1024)S(1)} %add_rsqrt_fusion.2), kind=kOutput, calls=%fused_computation.81 | convolution fusion | flops 29087760384 | bytes 23608320 | tf_op jit(solution)/shard_map/dot_general | solution.py:276
  345.4 4.4 multiply_reduce_fusion.8
  349.8 1.9 convolution_convert_fusion.3
  351.8 4.4 reshape_reshape.10
  356.1 3.0 copy.194
  359.2 46.4 %while.35 = (s32[]{:T(128)}, bf16[6,4,128,96]{2,1,0,3:T(4,128)(2,1)}, f32[6,4,12,128]{3,2,1,0:T(8,128)}, bf16[6,4,128,288]{2,3,1,0:T(8,128)(2,1)}, s32[6,4]{1,0:T(8,128)}, /*index=5*/f32[12,16384]{1,0:T(8,128)}, s32[]{:T(128)}) while((s32[]{:T(128)}, bf16[6,4,128,96]{2,1,0,3:T(4,128)(2,1)}, f32[6,4,12,128]{3,2,1,0:T(8,128)}, ...), condition=%wide.region_10.11_spmd, body=%wide.region_7.10_spmd.sunk | while | flops 34646528 | bytes 18443396 | solution.py:123
  361.1 1.4 copy.293
  368.8 1.4 copy.293
  376.5 1.4 copy.293
  399.6 1.4 copy.293
  405.5 1.6 reshape_reshape.11
  409.2 3.6 fusion.47
  412.8 1.5 multiply_reduce_fusion.3
  418.4 98.0 %while.36 = (s32[]{:T(128)}, bf16[6,4,128,288]{2,1,0,3:T(4,128)(2,1)}, f32[6,12,128,128]{2,3,1,0:T(8,128)}, bf16[6,4,128,288]{2,3,1,0:T(8,128)(2,1)}, s32[6,4]{1...) while((s32[]{:T(128)}, ...), condition=%wide.region_16.17_spmd, body=%wide.region_13.16_spmd.sunk | while | flops 72395264 | bytes 39774420 | solution.py:172
  424.9 2.3 copy.299
  427.1 2.5 multiply_reduce_fusion.13
  441.2 2.3 copy.299
  443.5 2.5 multiply_reduce_fusion.13
  457.5 2.3 copy.299
  459.8 2.5 multiply_reduce_fusion.13
  473.8 2.3 copy.299
  476.1 2.5 multiply_reduce_fusion.13
  490.1 2.3 copy.299
  492.4 2.5 multiply_reduce_fusion.13
  506.5 2.3 copy.299
  508.8 2.5 multiply_reduce_fusion.13
  516.5 3.4 reshape.359
  519.9 2.3 multiply_reduce_fusion.4
  523.0 5.2 fusion.72
  528.2 3.9 fusion.57
  534.9 3.1 fusion.60
  538.0 3.8 fusion.65
  543.8 2.7 reduce_sum.167
  548.9 122.7 %all-reduce.4.cloned.1.call-done = f32[184320]{0:T(1024)} async-done(((f32[184320]{0:T(1024)}), f32[184320]{0:T(1024)}) %all-reduce.4.cloned.1.call-update) | async-done | bytes 737296
  671.6 1.4 multiply_reduce_fusion.9
  673.0 2.9 copy_bitcast_fusion.14
  675.9 40.5 %all-reduce.1 = (f32[]{:T(128)}, f32[3,96]{1,0:T(4,128)S(1)}, f32[32,12]{0,1:T(8,128)S(1)}) all-reduce(f32[]{:T(128)} %multiply_reduce_fusion.9, f32[3,96]{1,0:T(4,128)S(1)} %pad_maximum_fusion.4, f32[32,12]{0,1:T(8,128)S(1)} %fusion.55), channel_id=1, replica_groups=mesh['batch'=8,'mp'=4] {'batch','mp'}, use_global_device_ids=true, to_apply=%region_20.21 | all-reduce | flops 673 | bytes 5384 | tf_op jit(solution)/shard_map/psum | solution.py:339
  722.4 1.5 fusion.96
  (598 shorter events, 236.1 us)
Async XLA Ops:
  7.2 288.4 %copy-start = (bf16[768,768]{1,0:T(8,128)(2,1)S(1)}, bf16[768,768]{1,0:T(8,128)(2,1)}, u32[]{:S(2)}) copy-start(bf16[768,768]{1,0:T(8,128)(2,1)} %param.31) | copy-start | bytes 3538948
  8.0 217.5 %collective-permute-start = (bf16[5760]{0:T(1024)(128)(2,1)S(1)}, bf16[5760]{0:T(1024)(128)(2,1)S(1)}, u32[]{:S(2)}, u32[]{:S(2)}) collective-permute-start(bf16[5760]{0:T(1024)(128)(2,1)S(1)} %convert_element_type.134), channel_id=1, source_target_pairs={{0,1},{1,0},{2,3},{3,2},{4,5},{5,4},{6,7},{7,6},{8,9},{9,8},{10,11... | collective-permute-start | bytes 34568 | tf_op jit(solution)/shard_map/ppermute | solution.py:248
  9.3 12.0 %copy-start.2 = (bf16[96,128,768]{2,1,0:T(8,128)(2,1)S(1)}, bf16[96,128,768]{2,1,0:T(8,128)(2,1)}, u32[]{:S(2)}) copy-start(bf16[96,128,768]{2,1,0:T(8,128)(2,1)} %param.27) | copy-start | bytes 56623108
  21.3 10.2 %copy-start.49 = (bf16[3,768,192]{1,2,0:T(8,128)(2,1)S(1)}, bf16[3,768,192]{1,2,0:T(8,128)(2,1)}, u32[]{:S(2)}) copy-start(bf16[3,768,192]{1,2,0:T(8,128)(2,1)} %param.30) | copy-start | bytes 2654212
  97.8 8.2 %copy-start.47 = (s32[96]{0:T(128)S(1)}, s32[96]{0:T(128)}, u32[]{:S(2)}) copy-start(s32[96]{0:T(128)} %param.28) | copy-start | bytes 1156
  97.8 8.3 %copy-start.24 = (s32[16384]{0:T(1024)S(1)}, s32[16384]{0:T(1024)}, u32[]{:S(2)}) copy-start(s32[16384]{0:T(1024)} %constant.99.clone) | copy-start | bytes 196612
  210.4 79.6 %all-to-all-start = ((bf16[96,128,192]{1,2,0:T(8,128)(2,1)}), bf16[96,128,192]{1,2,0:T(8,128)(2,1)}, u32[]{:S(2)}, u32[]{:S(2)}) async-start(bf16[96,128,192]{1,2,0:T(8,128)(2,1)} %bitcast.305), calls=%async_computation | async-start | bytes 9437184 | tf_op jit(solution)/shard_map/all_to_all | solution.py:267
  215.3 456.3 %all-reduce.4.cloned.1.call-start = ((), (), s32[]{:S(2)}) async-start(), calls=%async_computation.1 | async-start | bytes 1474560
  218.4 4.7 copy-start.32
  218.4 9.6 %copy-start.43 = (f32[3,96]{1,0:T(4,128)S(1)}, f32[3,96]{1,0:T(4,128)}, u32[]{:S(2)}) copy-start(f32[3,96]{1,0:T(4,128)} %param.40) | copy-start | bytes 3460
  225.5 44.9 %collective-permute-start.1 = (bf16[11520]{0:T(1024)(128)(2,1)S(1)}, bf16[11520]{0:T(1024)(128)(2,1)S(1)}, u32[]{:S(2)}, u32[]{:S(2)}) collective-permute-start(bf16[11520]{0:T(1024)(128)(2,1)S(1)} %maximum_select_fusion.13), channel_id=1, source_target_pairs={{0,2},{1,3},{2,0},{3,1},{4,6},{5,7},{6,4},{7,5},{8,10},{9,11},{10,... | collective-permute-start | bytes 69128 | tf_op jit(solution)/shard_map/ppermute | solution.py:248
  228.6 116.8 %copy-start.38 = (f32[1,96]{1,0:T(1,128)}, f32[1,96]{1,0:T(1,128)S(1)}, u32[]{:S(2)}) copy-start(f32[1,96]{1,0:T(1,128)S(1)} %get-tuple-element.450) | copy-start | bytes 1156
  228.6 116.8 %copy-start.40 = (f32[96]{0:T(128)}, f32[96]{0:T(128)S(1)}, u32[]{:S(2)}) copy-start(f32[96]{0:T(128)S(1)} %get-tuple-element.449) | copy-start | bytes 1156
  228.6 121.2 %copy-start.35 = (f32[96]{0:T(128)}, f32[96]{0:T(128)S(1)}, u32[]{:S(2)}) copy-start(f32[96]{0:T(128)S(1)} %get-tuple-element.448) | copy-start | bytes 1156
  270.5 4.1 collective-permute-start.2
  274.6 4.6 collective-permute-start.3
  279.3 9.1 %collective-permute-start.4 = (bf16[92160]{0:T(1024)(128)(2,1)S(1)}, bf16[92160]{0:T(1024)(128)(2,1)S(1)}, u32[]{:S(2)}, u32[]{:S(2)}) collective-permute-start(bf16[92160]{0:T(1024)(128)(2,1)S(1)} %maximum_select_fusion.3), channel_id=1, source_target_pairs={{0,16},{1,17},{2,18},{3,19},{4,20},{5,21},{6,22},{7,23},{8,24},{9,... | collective-permute-start | bytes 552968 | tf_op jit(solution)/shard_map/ppermute | solution.py:248
  289.1 60.8 %copy-start.18 = (bf16[96,288]{1,0:T(8,128)(2,1)}, bf16[96,288]{1,0:T(8,128)(2,1)S(1)}, u32[]{:S(2)}) copy-start(bf16[96,288]{1,0:T(8,128)(2,1)S(1)} %fusion.78) | copy-start | bytes 165892
  289.9 126.1 %copy-start.17 = (bf16[1920,96]{1,0:T(8,128)(2,1)}, bf16[1920,96]{1,0:T(8,128)(2,1)S(1)}, u32[]{:S(2)}) copy-start(bf16[1920,96]{1,0:T(8,128)(2,1)S(1)} %maximum_select_fusion) | copy-start | bytes 1105924
  290.0 5.6 copy-start.9
  302.5 42.8 %copy-start.10 = (f32[24,128,96]{1,2,0:T(8,128)S(1)}, f32[24,128,96]{1,2,0:T(8,128)}, u32[]{:S(2)}) copy-start(f32[24,128,96]{1,2,0:T(8,128)} %param.35) | copy-start | bytes 3538948
  349.8 57.3 %copy-start.3 = (f32[3072,96]{0,1:T(8,128)}, f32[3072,96]{0,1:T(8,128)S(1)}, u32[]{:S(2)}) copy-start(f32[3072,96]{0,1:T(8,128)S(1)} %get-tuple-element.435) | copy-start | bytes 3538948
  405.5 2.0 copy-start.20
  405.5 2.0 copy-start.37
  407.5 8.1 %copy-start.5 = (f32[3072,96]{0,1:T(8,128)}, f32[3072,96]{0,1:T(8,128)S(1)}, u32[]{:S(2)}) copy-start(f32[3072,96]{0,1:T(8,128)S(1)} %get-tuple-element.455) | copy-start | bytes 3538948
  407.5 1.7 copy-start.15
  407.5 1.7 copy-start.30
  409.2 3.6 copy-start.11
  418.4 1.2 copy-start.12
  432.0 2.8 copy-start.13
  434.8 1.2 copy-start.12
  448.3 2.8 copy-start.13
  451.1 1.2 copy-start.12
  464.6 2.8 copy-start.13
  467.4 1.2 copy-start.12
  480.9 2.8 copy-start.13
  483.7 1.2 copy-start.12
  497.2 2.8 copy-start.13
  500.1 1.2 copy-start.12
  513.6 2.9 copy-start.13
  516.4 3.4 copy-start.4
  516.4 3.4 copy-start.19
  516.4 3.4 copy-start.36
  519.8 3.1 copy-start.16
  519.9 3.1 copy-start.31
  522.1 6.0 slice-start
  522.9 5.2 copy-start.6
  523.0 5.2 slice-start.1
  528.2 4.5 copy-start.21
  528.2 5.2 copy-start.27
  528.2 6.7 copy-start.8
  534.9 3.1 copy-start.41
  537.9 4.2 copy-start.26
  538.0 4.3 copy-start.23
  538.0 4.3 copy-start.28
  538.0 4.4 copy-start.22
  541.8 1.5 copy-start.39
  541.8 1.4 copy-start.46
  546.6 1.1 copy-start.25
  546.9 176.9 %copy-start.1 = (bf16[768,768]{1,0:T(8,128)(2,1)S(1)}, bf16[768,768]{1,0:T(8,128)(2,1)}, u32[]{:S(2)}) copy-start(bf16[768,768]{1,0:T(8,128)(2,1)} %param.31) | copy-start | bytes 3538948
  547.6 172.1 %copy-start.33 = (f32[32,12]{0,1:T(8,128)S(1)}, f32[32,12]{0,1:T(8,128)}, u32[]{:S(2)}) copy-start(f32[32,12]{0,1:T(8,128)} %param.43) | copy-start | bytes 4612
  547.6 172.1 %copy-start.42 = (f32[32,12]{0,1:T(8,128)S(1)}, f32[32,12]{0,1:T(8,128)}, u32[]{:S(2)}) copy-start(f32[32,12]{0,1:T(8,128)} %param.45) | copy-start | bytes 4612
  547.6 174.8 %copy-start.29 = (f32[5760]{0:T(1024)S(1)}, f32[5760]{0:T(1024)}, u32[]{:S(2)}) copy-start(f32[5760]{0:T(1024)} %param.37) | copy-start | bytes 69124
  547.6 174.8 %copy-start.34 = (f32[5760]{0:T(1024)S(1)}, f32[5760]{0:T(1024)}, u32[]{:S(2)}) copy-start(f32[5760]{0:T(1024)} %param.39) | copy-start | bytes 69124
  (5 other events, 4.9 us)
Sparse Core Ops, SparseCore 0:
  543.4 128.1 all-reduce.3
